TPU v7x, 512 devices: a whole 4x4x16 slice. The times are simulated.
512 devices in a mesh: dp: 4 (over y), head: 2 (over core), tile: 64 (over z, x).
Axes of the slice: x: 4, y: 4, z: 16, core: 2. Of those that a mesh axis runs over, the one named last changes fastest.
Arguments:
- tiles_in: bfloat16 [4, 16384, 2560], P('dp', 'tile'), may hold values from -6 to 6
- key_weight: bfloat16 [2560, 1280], P('tile', 'head'), may hold values from -0.125 to 0.125
- value_weight: bfloat16 [2560, 1280], P('tile', 'head'), may hold values from -0.125 to 0.125
- queries: bfloat16 [512, 1280], P(None, 'head'), may hold values from -300 to 300
- out_grad: bfloat16 [4, 512, 1280], P('dp', None, 'head'), may hold values from -1536 to 1536
- valid_count: int32 [4], P('dp'), may hold values from 4096 to 16384, as said below
- tile_mask: int32 [4, 16384], P('dp', 'tile'), may hold values 0 or 1
Outputs:
- tile_grad: bfloat16 [4, 16384, 2560], P('dp', 'tile', 'head')
Inputs may be any that keep to these rules, and one draw needn't show every extreme that they name: Some slide has valid_count equal to 16384.
All inputs are finite; a program needn't handle non-finite values. No bound on the sum of `tile_mask` on one device may be relied on, other than what follows from the above.
Results may differ from a plain program's by a relative error of at most 0.022.
Values may be sent and summed in bfloat16 or wider, within the bound.
No kernel may reach another device: no remote copies, remote signals or barrier semaphores. Data moves between devices by JAX's collectives and lax.ppermute only.
A program may use at most 64 MiB of HBM per device.

v0:
```python
import jax
import jax.numpy as jnp
from jax import lax
from jax.sharding import PartitionSpec as P

HDIM = 80
NEG_LARGE = -1e30


def per_device(tiles_in, key_weight, value_weight, queries, out_grad, valid_count, tile_mask):
    inv_scale = HDIM ** (-0.5)
    tile_dev = tiles_in.shape[1]
    group_width = queries.shape[1]
    heads_here = group_width // HDIM
    latents = queries.shape[0]
    local_tiles = tiles_in[0]
    positions = lax.axis_index("tile") * tile_dev + jnp.arange(tile_dev, dtype=jnp.int32)
    kept = (tile_mask[0] == 1) | (positions == 0)
    valid = ((positions < valid_count[0]) & kept)[None, None, :]
    full_key, full_value = (
        lax.all_gather(key_weight, "tile", axis=0, tiled=True),
        lax.all_gather(value_weight, "tile", axis=0, tiled=True),
    )
    keys = jnp.dot(local_tiles, full_key, preferred_element_type=jnp.float32)
    values = jnp.dot(local_tiles, full_value, preferred_element_type=jnp.float32).astype(
        jnp.bfloat16
    )
    query_heads = queries.reshape(latents, heads_here, HDIM)
    query_wide = queries.astype(jnp.float32).reshape(latents, heads_here, HDIM)
    key_heads = keys.reshape(tile_dev, heads_here, HDIM)
    value_heads = values.reshape(tile_dev, heads_here, HDIM)
    grad_heads = out_grad[0].reshape(latents, heads_here, HDIM)
    scores = (
        jnp.einsum(
            "lhd,thd->hlt",
            query_wide,
            key_heads,
            precision=lax.Precision.HIGHEST,
            preferred_element_type=jnp.float32,
        )
        * inv_scale
    )
    prob_grad = jnp.einsum(
        "lhd,thd->hlt", grad_heads, value_heads, preferred_element_type=jnp.float32
    )
    local_max = jnp.max(jnp.where(valid, scores, NEG_LARGE), axis=2)
    row_max = lax.pmax(local_max, "tile")
    expd = jnp.where(valid, jnp.exp(scores - row_max[:, :, None]), 0.0)
    total, weighted = lax.psum((jnp.sum(expd, axis=2), jnp.sum(expd * prob_grad, axis=2)), "tile")
    delta = weighted / total
    probs = expd / total[:, :, None]
    dscore = (inv_scale * probs * (prob_grad - delta[:, :, None])).astype(jnp.bfloat16)
    value_grad = (
        jnp.einsum(
            "hlt,lhd->thd",
            probs.astype(jnp.bfloat16),
            grad_heads,
            preferred_element_type=jnp.float32,
        )
        .astype(jnp.bfloat16)
        .reshape(tile_dev, group_width)
    )
    key_grad = (
        jnp.einsum("hlt,lhd->thd", dscore, query_heads, preferred_element_type=jnp.float32)
        .astype(jnp.bfloat16)
        .reshape(tile_dev, group_width)
    )
    partial_sum = jnp.einsum("tc,rc->tr", key_grad, full_key, preferred_element_type=jnp.float32)
    partial_sum = partial_sum + jnp.einsum(
        "tc,rc->tr", value_grad, full_value, preferred_element_type=jnp.float32
    )
    rounded = partial_sum.astype(jnp.bfloat16)
    summed = lax.psum_scatter(rounded[None], "head", scatter_dimension=2, tiled=True).astype(
        jnp.float32
    )
    return summed.astype(jnp.bfloat16)


def solution(mesh):
    return jax.shard_map(
        per_device,
        mesh=mesh,
        in_specs=(
            P("dp", "tile", None),
            P("tile", "head"),
            P("tile", "head"),
            P(None, "head"),
            P("dp", None, "head"),
            P("dp"),
            P("dp", "tile"),
        ),
        out_specs=P("dp", "tile", "head"),
        check_vma=False,
    )
```

profile of v0, /device:TPU:1, one launch (start us, length us, event | category | flops | bytes accessed | tf_op | source)
XLA Modules:
  0.0 901.9 jit_solution(17040804668018746320)
XLA Ops:
  6.5 0.7 all-gather.5.cloned.1.call-update
  7.3 0.7 all-gather.3.cloned.1.call-update
  8.0 0.0 reduce-scatter.2.cloned.1.call-start
  8.7 1.3 copy.22
  10.0 1.3 copy.24
  11.4 0.7 compare_reduce_fusion
  12.1 139.2 %all-gather.5.cloned.1.call-done = bf16[2560,640]{1,0:T(8,128)(2,1)} async-done(((bf16[40,640]{1,0:T(8,128)(2,1)}), bf16[2560,640]{1,0:T(8,128)(2,1)}) %all-gather.5.cloned.1.call-update) | async-done | bytes 3276816 | tf_op jit(solution)/shard_map/all_gather | solution.py:22
  151.3 3.1 fusion.15
  154.4 0.2 copy.23
  154.6 138.5 %all-gather.3.cloned.1.call-done = bf16[2560,640]{1,0:T(8,128)(2,1)} async-done(((bf16[40,640]{1,0:T(8,128)(2,1)}), bf16[2560,640]{1,0:T(8,128)(2,1)}) %all-gather.3.cloned.1.call-update) | async-done | bytes 3276816 | tf_op jit(solution)/shard_map/all_gather | solution.py:21
  293.1 5.7 copy.21
  298.8 3.0 fusion.11
  301.8 4.2 select_reduce_fusion
  305.9 221.1 %pmax.7 = f32[8,512]{1,0:T(8,128)S(1)} all-reduce(f32[8,512]{1,0:T(8,128)S(1)} %get-tuple-element.9), channel_id=1, replica_groups=mesh['dp'=4,'head'=2,'tile'=64] {'tile'}, use_global_device_ids=true, to_apply=%region_1.2 | all-reduce | flops 4096 | bytes 32768 | tf_op jit(solution)/shard_map/pmax | solution.py:47
  527.0 5.7 bitcast_reduce_fusion
  532.7 219.7 %all-reduce = (f32[8,512]{1,0:T(8,128)S(1)}, f32[8,512]{1,0:T(8,128)S(1)}) all-reduce(f32[8,512]{1,0:T(8,128)S(1)} %get-tuple-element.6, f32[8,512]{1,0:T(8,128)S(1)} %get-tuple-element.5), channel_id=1, replica_groups=mesh['dp'=4,'head'=2,'tile'=64] {'tile'}, use_global_device_ids=true, to_apply=%region_5.6 | all-reduce | flops 8192 | bytes 65536 | tf_op jit(solution)/shard_map/psum | solution.py:49
  752.4 3.5 fusion.18
  755.9 1.2 copy-done.3
  757.1 1.6 fusion.21
  758.7 0.4 copy-done.2
  759.0 1.2 fusion.25
  760.3 0.4 copy-done.4
  760.7 2.4 fusion.4
  763.1 132.3 %reduce-scatter.2.cloned.1.call-done = bf16[1,256,1280]{2,1,0:T(8,128)(2,1)} async-done(((bf16[1,256,2560]{2,1,0:T(8,128)(2,1)}), bf16[1,256,1280]{2,1,0:T(8,128)(2,1)}) %reduce-scatter.2.cloned.1.call-update) | async-done | bytes 655376 | tf_op jit(solution)/shard_map/reduce_scatter | solution.py:73
  (12 shorter events, 0.1 us)
Async XLA Ops:
  6.5 144.7 %copy-start = (bf16[1,256,2560]{2,1,0:T(8,128)(2,1)S(1)}, bf16[1,256,2560]{2,1,0:T(8,128)(2,1)}, u32[]{:S(2)}) copy-start(bf16[1,256,2560]{2,1,0:T(8,128)(2,1)} %param.7) | copy-start | bytes 3932164
  6.5 144.7 %all-gather.5.cloned.1.call-start = ((), (), s32[]{:S(2)}) async-start(), calls=%async_computation.2 | async-start | bytes 3328000 | tf_op jit(solution)/shard_map/all_gather | solution.py:22
  7.3 285.8 %all-gather.3.cloned.1.call-start = ((), (), s32[]{:S(2)}) async-start(), calls=%async_computation.1 | async-start | bytes 3328000 | tf_op jit(solution)/shard_map/all_gather | solution.py:21
  8.0 887.3 %reduce-scatter.2.cloned.1.call-start = ((), (), s32[]{:S(2)}) async-start(), calls=%async_computation.3 | async-start | bytes 1966080 | tf_op jit(solution)/shard_map/reduce_scatter | solution.py:73
  752.4 3.5 copy-start.1
  752.4 4.7 copy-start.3
  757.1 1.9 copy-start.2
  758.7 2.0 copy-start.4
Sparse Core Ops, SparseCore 0:
  10.3 140.9 all-gather.4
  154.2 138.8 all-gather.2
  763.2 132.0 reduce-scatter.1
where the time goes:
time: 902 us
  blocking collectives  441 us (49%)
  waiting for transfers between devices  411 us (46%)
  matrix products  24.5 us (3%)
  between operations  13.8 us (2%)
  local copies, waits for them, and re-layouts  10.5 us (1%)
    pmax x1, blocking collectives, per_device(): row_max = lax.pmax(local_max, 'tile')  221 us
    psum x1, blocking collectives, per_device(): lax.psum((jnp.sum(expd, axis=2), jnp.sum(expd * prob_grad, axis=2)), 'tile')  220 us
    all_gather x1, waiting for transfers between devices, per_device(): lax.all_gather(value_weight, 'tile', axis=0, tiled=True)  139 us
    all_gather x1, waiting for transfers between devices, per_device(): lax.all_gather(key_weight, 'tile', axis=0, tiled=True)  139 us
    reduce_scatter x1, waiting for transfers between devices, per_device(): lax.psum_scatter(rounded[None], 'head', scatter_dimension=2, tiled=True)  132 us
  transfers between devices with their start and end apart: 3, of which 3 were waited for; matrix products, arithmetic and copies ran while one was open for 1% of the time, Pallas kernels for 0%

commit v1 on v0

--- a/solution.py
+++ b/solution.py
@@ -2,6 +2,7 @@
 import jax.numpy as jnp
 from jax import lax
 from jax.sharding import PartitionSpec as P
+from jax.lax import all_to_all, axis_size
 
 HDIM = 80
 NEG_LARGE = -1e30
@@ -19,7 +20,15 @@
     valid = ((positions < valid_count[0]) & kept)[None, None, :]
     full_key, full_value = (
         lax.all_gather(key_weight, "tile", axis=0, tiled=True),
-        lax.all_gather(value_weight, "tile", axis=0, tiled=True),
+        jnp.concatenate(
+            all_to_all(
+                jnp.stack([value_weight] * axis_size("tile"), axis=0),
+                axis_name="tile",
+                split_axis=0,
+                concat_axis=0,
+            ),
+            axis=0,
+        ),
     )
     keys = jnp.dot(local_tiles, full_key, preferred_element_type=jnp.float32)
     values = jnp.dot(local_tiles, full_value, preferred_element_type=jnp.float32).astype(

time: 902 us -> 825 us (0.915)
  waiting for transfers between devices: 411 us -> 311 us
  starting transfers between devices: 0.08 us -> 19.6 us
    all_gather x1 -> x0, waiting for transfers between devices: 139 us -> none  [per_device(): lax.all_gather(value_weight, 'tile', axis=0, tiled=True)]
    all_gather x1, waiting for transfers between devices: 139 us -> 180 us  [per_device(): lax.all_gather(key_weight, 'tile', axis=0, tiled=True)]
    all_to_all x0 -> x1, starting transfers between devices: none -> 19.5 us  [per_device(): all_to_all(jnp.stack([value_weight] * axis_size('tile'), axis=0), axis_na...]
  transfers between devices with their start and end apart: 3 -> 3, of which waited for: 3 -> 2; matrix products, arithmetic and copies ran while one was open for 1% -> 2% of each run, Pallas kernels for 0% -> 0%
where the time goes in v1:
time: 825 us
  blocking collectives  442 us (54%)
  waiting for transfers between devices  311 us (38%)
  matrix products  26.5 us (3%)
  starting transfers between devices  19.6 us (2%)
  between operations  14.2 us (2%)
  local copies, waits for them, and re-layouts  10.9 us (1%)
    pmax x1, blocking collectives, per_device(): row_max = lax.pmax(local_max, 'tile')  223 us
    psum x1, blocking collectives, per_device(): lax.psum((jnp.sum(expd, axis=2), jnp.sum(expd * prob_grad, axis=2)), 'tile')  220 us
    all_gather x1, waiting for transfers between devices, per_device(): lax.all_gather(key_weight, 'tile', axis=0, tiled=True)  180 us
    reduce_scatter x1, waiting for transfers between devices, per_device(): lax.psum_scatter(rounded[None], 'head', scatter_dimension=2, tiled=True)  130 us
    all_to_all x1, starting transfers between devices, per_device(): all_to_all(jnp.stack([value_weight] * axis_size('tile'), axis=0), axis_na...  19.5 us
  transfers between devices with their start and end apart: 3, of which 2 were waited for; matrix products, arithmetic and copies ran while one was open for 2% of the time, Pallas kernels for 0%

profile of v1, /device:TPU:1, one launch (start us, length us, event | category | flops | bytes accessed | tf_op | source)
XLA Modules:
  0.0 824.7 jit_solution(8546799551818420046)
XLA Ops:
  6.5 2.9 stack.2
  9.5 19.5 %all-to-all-start = ((bf16[64,40,640]{2,1,0:T(8,128)(2,1)}), bf16[64,40,640]{2,1,0:T(8,128)(2,1)}, u32[]{:S(2)}, u32[]{:S(2)}) async-start(bf16[64,40,640]{2,1,0:T(8,128)(2,1)} %stack.2), calls=%async_computation | async-start | bytes 6553600 | tf_op jit(solution)/shard_map/all_to_all | solution.py:24
  28.9 0.0 all-gather.2.cloned.1.call-start
  29.0 0.7 all-gather.2.cloned.1.call-update
  29.7 0.0 reduce-scatter.2.cloned.1.call-start
  30.4 0.3 copy.22
  30.6 0.3 copy.24
  31.0 180.3 %all-gather.2.cloned.1.call-done = bf16[2560,640]{1,0:T(8,128)(2,1)} async-done(((bf16[40,640]{1,0:T(8,128)(2,1)}), bf16[2560,640]{1,0:T(8,128)(2,1)}) %all-gather.2.cloned.1.call-update) | async-done | bytes 3276816 | tf_op jit(solution)/shard_map/all_gather | solution.py:22
  211.3 5.7 copy.21
  217.0 3.0 fusion.11
  219.9 4.2 select_reduce_fusion
  224.1 222.8 %pmax.7 = f32[8,512]{1,0:T(8,128)S(1)} all-reduce(f32[8,512]{1,0:T(8,128)S(1)} %get-tuple-element.9), channel_id=1, replica_groups=mesh['dp'=4,'head'=2,'tile'=64] {'tile'}, use_global_device_ids=true, to_apply=%region_1.2 | all-reduce | flops 4096 | bytes 32768 | tf_op jit(solution)/shard_map/pmax | solution.py:56
  446.9 3.1 fusion.15
  450.0 0.2 copy.23
  450.2 5.7 bitcast_reduce_fusion
  455.9 219.6 %all-reduce = (f32[8,512]{1,0:T(8,128)S(1)}, f32[8,512]{1,0:T(8,128)S(1)}) all-reduce(f32[8,512]{1,0:T(8,128)S(1)} %get-tuple-element.6, f32[8,512]{1,0:T(8,128)S(1)} %get-tuple-element.5), channel_id=1, replica_groups=mesh['dp'=4,'head'=2,'tile'=64] {'tile'}, use_global_device_ids=true, to_apply=%region_5.6 | all-reduce | flops 8192 | bytes 65536 | tf_op jit(solution)/shard_map/psum | solution.py:58
  675.5 3.5 fusion.18
  679.0 1.2 copy-done.3
  680.2 1.6 fusion.21
  681.8 0.4 copy-done.2
  682.1 1.2 fusion.25
  683.4 4.3 fusion.4
  687.7 0.0 reduce-scatter.2.cloned.1.call-update
  687.7 130.2 %reduce-scatter.2.cloned.1.call-done = bf16[1,256,1280]{2,1,0:T(8,128)(2,1)} async-done(((bf16[1,256,2560]{2,1,0:T(8,128)(2,1)}), bf16[1,256,1280]{2,1,0:T(8,128)(2,1)}) %reduce-scatter.2.cloned.1.call-update) | async-done | bytes 655376 | tf_op jit(solution)/shard_map/reduce_scatter | solution.py:82
  (16 shorter events, 0.1 us)
Async XLA Ops:
  6.5 210.4 %copy-start = (bf16[1,256,2560]{2,1,0:T(8,128)(2,1)S(1)}, bf16[1,256,2560]{2,1,0:T(8,128)(2,1)}, u32[]{:S(2)}) copy-start(bf16[1,256,2560]{2,1,0:T(8,128)(2,1)} %param.7) | copy-start | bytes 3932164
  6.5 23.8 %copy-start.4 = (bf16[512,640]{1,0:T(8,128)(2,1)S(1)}, bf16[512,640]{1,0:T(8,128)(2,1)}, u32[]{:S(2)}) copy-start(bf16[512,640]{1,0:T(8,128)(2,1)} %param.10) | copy-start | bytes 1966084
  9.4 21.2 %copy-start.5 = (bf16[1,512,640]{2,1,0:T(8,128)(2,1)S(1)}, bf16[1,512,640]{2,1,0:T(8,128)(2,1)}, u32[]{:S(2)}) copy-start(bf16[1,512,640]{2,1,0:T(8,128)(2,1)} %param.11) | copy-start | bytes 1966084
  9.5 21.5 %copy-start.6 = (s32[1,256]{1,0:T(1,128)S(1)}, s32[1,256]{1,0:T(1,128)}, u32[]{:S(2)}) copy-start(s32[1,256]{1,0:T(1,128)} %param.13) | copy-start | bytes 3076
  9.5 437.5 %all-to-all-start = ((bf16[64,40,640]{2,1,0:T(8,128)(2,1)}), bf16[64,40,640]{2,1,0:T(8,128)(2,1)}, u32[]{:S(2)}, u32[]{:S(2)}) async-start(bf16[64,40,640]{2,1,0:T(8,128)(2,1)} %stack.2), calls=%async_computation | async-start | bytes 6553600 | tf_op jit(solution)/shard_map/all_to_all | solution.py:24
  28.9 182.3 %all-gather.2.cloned.1.call-start = ((), (), s32[]{:S(2)}) async-start(), calls=%async_computation.2 | async-start | bytes 3328000 | tf_op jit(solution)/shard_map/all_gather | solution.py:22
  29.7 788.2 %reduce-scatter.2.cloned.1.call-start = ((), (), s32[]{:S(2)}) async-start(), calls=%async_computation.3 | async-start | bytes 1966080 | tf_op jit(solution)/shard_map/reduce_scatter | solution.py:82
  675.5 3.5 copy-start.1
  675.5 4.7 copy-start.3
  680.2 1.9 copy-start.2
Sparse Core Ops, SparseCore 0:
  32.7 178.5 all-gather.1
  687.8 130.0 reduce-scatter.1
